TPU v7x, 128 devices: a whole 4x4x4 slice. The times are simulated.
128 devices in a mesh: front: 8 (over x, core), grp: 16 (over y, z).
Axes of the slice: x: 4, y: 4, z: 4, core: 2. Of those that a mesh axis runs over, the one named last changes fastest.
Arguments:
- contributions: bfloat16 [16384, 16384], P(('front', 'grp')), may hold values from -6 to 6
- sketch_matrix: bfloat16 [16384, 256], P(('front', 'grp')), may hold values from -0.046875 to 0.046875
- destinations: int32 [16384, 1], replicated, may hold values from 0 to 127; in each aligned block of 128 rows (0 to 127, 128 to 255, ...) at most 2 rows name the same one
- parent_rows: int32 [16384], replicated, may hold values from 0 to 1023
- front_sizes: int32 [8], P('front'), may hold values from 8192 to 16384
- leaf_skeleton: int32 [8, 16, 128], P('front', 'grp'), may hold values from 0 to 1023, as said below
- merge_skeleton: int32 [8, 14, 128], P('front'), may hold values from 0 to 255, as said below
Outputs:
- leaf_maps: float32 [8, 16384, 128], P('front', 'grp')
- node_maps: float32 [8, 16, 3, 256, 128], P('front', 'grp')
- top_rows: float32 [8, 16, 128, 256], P('front', 'grp')
Inputs may be any that keep to these rules, and one draw needn't show every extreme that they name: `destinations`: in the rows of one device no destination is named by more than 2 rows. `leaf_skeleton`: each row holds 128 different row numbers of a leaf block. `merge_skeleton`: each row holds 128 different positions of the stacked 2 * 128 rows.
All inputs are finite; a program needn't handle non-finite values.
Results may differ from a plain program's by a relative error of at most 0.003.
Values may be sent and summed in bfloat16 or wider, within the bound.
No kernel may reach another device: no remote copies, remote signals or barrier semaphores. Data moves between devices by JAX's collectives and lax.ppermute only.
A program may use at most 64 MiB of HBM per device.

v0:
```python
import jax
import jax.numpy as jnp
from jax import lax
from jax.sharding import PartitionSpec as P

PR_DEV = 1024
LEVELS = 3


def from_partner(block, axis, stride):
    count = lax.axis_size(axis)
    route = []
    for low in range(count):
        high = low | 1 << stride
        if high != low and high < count:
            route += [(low, high), (high, low)]
    return lax.ppermute(block, axis, route)


def ridge_map(rows, basis):
    gram = jnp.dot(basis, basis.T, precision=lax.Precision.HIGHEST)
    shift = 0.1 * jnp.mean(jnp.diagonal(gram)) + 1e-05
    ident = jnp.eye(gram.shape[0], dtype=jnp.float32)
    gram = gram + shift * ident
    approx = ident / jnp.trace(gram)
    for step in range(24):
        approx = jnp.dot(
            approx,
            2.0 * ident - jnp.dot(gram, approx, precision=lax.Precision.HIGHEST),
            precision=lax.Precision.HIGHEST,
        )
    right = jnp.dot(rows, basis.T, precision=lax.Precision.HIGHEST)
    return jnp.dot(right, approx, precision=lax.Precision.HIGHEST)


def select_rows(rows, index):
    picker = (index[:, None] == jnp.arange(rows.shape[0], dtype=jnp.int32)[None, :]).astype(
        jnp.float32
    )
    return jnp.dot(picker, rows, precision=lax.Precision.HIGHEST)


def local(
    contributions,
    sketch_matrix,
    destinations,
    parent_rows,
    front_sizes,
    leaf_skeleton,
    merge_skeleton,
):
    fronts = lax.axis_size("front")
    leaves = lax.axis_size("grp")
    devices = fronts * leaves
    grp_index = lax.axis_index("grp")
    myself = lax.axis_index("front") * leaves + grp_index
    rows_dev = contributions.shape[0]
    width = sketch_matrix.shape[1]
    capacity = 2 * rows_dev // devices
    sketch = jnp.dot(
        contributions,
        lax.all_gather(sketch_matrix, ("front", "grp"), axis=0, tiled=True),
        preferred_element_type=jnp.float32,
    )
    sketch = sketch.astype(jnp.bfloat16)
    every_dest = destinations[:, 0].reshape(devices, rows_dev)
    every_row = parent_rows.reshape(devices, rows_dev)
    mine = lax.dynamic_index_in_dim(every_dest, myself, 0, keepdims=False)
    owners = jnp.arange(devices, dtype=jnp.int32)
    hits = (mine[:, None] == owners[None, :]).astype(jnp.int32)
    before = jnp.cumsum(hits, axis=0) - hits
    slot_of = jnp.sum(before * hits, axis=1)
    keys = mine * capacity + slot_of
    placing = (keys[None, :] == jnp.arange(devices * capacity, dtype=jnp.int32)[:, None]).astype(
        jnp.bfloat16
    )
    packed = jnp.dot(placing, sketch, preferred_element_type=jnp.float32).astype(jnp.bfloat16)
    packed = packed.reshape(devices, capacity, width)
    arrived = lax.all_to_all(
        packed, ("front", "grp"), split_axis=0, concat_axis=0, tiled=True
    ).reshape(devices * capacity, width)
    landing = (every_dest == myself).astype(jnp.int32)
    slots = jnp.cumsum(landing, axis=1) - landing
    match = landing[:, None, :] * (
        slots[:, None, :] == jnp.arange(capacity, dtype=jnp.int32)[None, :, None]
    ).astype(jnp.int32)
    local_row = jnp.sum(match * every_row[:, None, :], axis=2)
    filled = jnp.sum(match, axis=2)
    where_to = jnp.where(filled > 0, local_row, -1).reshape(devices * capacity)
    adding = (jnp.arange(PR_DEV, dtype=jnp.int32)[:, None] == where_to[None, :]).astype(
        jnp.bfloat16
    )
    parent = jnp.dot(adding, arrived, preferred_element_type=jnp.float32)
    global_row = grp_index * PR_DEV + jnp.arange(PR_DEV, dtype=jnp.int32)
    parent = jnp.where((global_row < front_sizes[0])[:, None], parent, jnp.zeros_like(parent))
    basis = select_rows(parent, leaf_skeleton[0, 0])
    leaf_map = ridge_map(parent, basis)
    skeletons = merge_skeleton[0]
    level_maps = []
    current = basis
    for level in range(LEVELS):
        partner = from_partner(current, "grp", level)
        upper_side = grp_index >> level & 1 == 1
        first = jnp.where(upper_side, partner, current)
        second = jnp.where(upper_side, current, partner)
        stacked = jnp.concatenate([first, second], axis=0)
        node = leaves - (leaves >> level) + (grp_index >> level + 1)
        chosen = lax.dynamic_index_in_dim(skeletons, node, 0, keepdims=False)
        current = select_rows(stacked, chosen)
        level_maps.append(ridge_map(stacked, current))
    node_maps = jnp.stack(level_maps, axis=0)
    return (leaf_map[None], node_maps[None, None], current[None, None])


def solution(mesh):
    in_specs = (
        P(("front", "grp"), None),
        P(("front", "grp"), None),
        P(),
        P(),
        P("front"),
        P("front", "grp", None),
        P("front", None, None),
    )
    out_specs = (
        P("front", "grp", None),
        P("front", "grp", None, None, None),
        P("front", "grp", None, None),
    )
    return jax.shard_map(local, mesh=mesh, in_specs=in_specs, out_specs=out_specs, check_vma=False)
```

profile of v0, /device:TPU:1, one launch (start us, length us, event | category | flops | bytes accessed | tf_op | source)
XLA Modules:
  0.0 180.9 jit_solution(4281349015124919198)
XLA Ops:
  7.2 0.7 all-gather.2.cloned.1.call-update
  7.9 0.9 copy.16
  9.1 0.7 fusion.47
  11.1 1.0 select_reduce_fusion
  12.1 0.7 fusion.46
  12.8 71.7 %all-gather.2.cloned.1.call-done = bf16[16384,256]{1,0:T(8,128)(2,1)} async-done(((bf16[128,256]{1,0:T(8,128)(2,1)}), bf16[16384,256]{1,0:T(8,128)(2,1)}) %all-gather.2.cloned.1.call-update) | async-done | bytes 8388624 | tf_op jit(solution)/shard_map/all_gather | solution.py:62
  84.5 6.1 %convolution_convert_fusion = bf16[256,256]{1,0:T(8,128)(2,1)S(1)} fusion(bf16[128,16384]{1,0:T(8,128)(2,1)} %param.7, bf16[16384,256]{1,0:T(8,128)(2,1)} %all-gather.2.cloned.1.call-done, s32[128]{0:T(128)S(1)} %fusion.46), kind=kOutput, calls=%fused_computation.102 | convolution fusion | flops 1090650112 | bytes 12714496 | tf_op jit(solution)/shard_map/dot_general | solution.py:77
  90.6 0.7 reshape.69
  91.3 5.4 %all-to-all-start = ((bf16[128,2,256]{2,1,0:T(2,128)(2,1)}), bf16[128,2,256]{2,1,0:T(2,128)(2,1)S(1)}, u32[]{:S(2)}, u32[]{:S(2)}) async-start(bf16[128,2,256]{2,1,0:T(2,128)(2,1)} %reshape.69), calls=%async_computation | async-start | bytes 262144 | tf_op jit(solution)/shard_map/all_to_all | solution.py:79
  97.0 0.7 fusion.43
  97.7 9.0 %all-to-all-done = bf16[128,2,256]{2,1,0:T(2,128)(2,1)S(1)} async-done(((bf16[128,2,256]{2,1,0:T(2,128)(2,1)}), bf16[128,2,256]{2,1,0:T(2,128)(2,1)S(1)}, u32[]{:S(2)}, u32[]{:S(2)}) %all-to-all-start) | async-done | bytes 131104 | tf_op jit(solution)/shard_map/all_to_all | solution.py:79
  106.8 0.3 convolution_select_fusion
  107.1 0.6 fusion.1
  107.7 0.8 collective-permute-start
  108.5 0.3 fusion.63
  108.8 1.0 fusion.62
  109.8 1.2 gather_fusion
  111.0 0.6 reduce_sum.97
  112.3 0.6 select_reduce_fusion.4
  113.6 0.2 select_subtract_fusion.95
  123.8 1.4 convolution_bitcast_fusion
  125.2 0.3 fusion.8
  125.5 0.3 fusion.87
  125.7 0.4 fusion.7
  126.1 1.4 collective-permute-start.1
  127.5 1.2 gather_fusion.1
  128.7 0.6 reduce_sum.99
  130.0 0.6 select_reduce_fusion.3
  131.3 0.2 select_subtract_fusion.71
  141.5 0.3 convolution_bitcast_fusion.3
  141.8 0.3 fusion.6
  142.1 0.3 fusion.111
  142.4 0.4 fusion.5
  142.7 0.7 collective-permute-start.2
  143.5 1.2 gather_fusion.2
  144.7 0.6 reduce_sum.101
  146.0 0.6 select_reduce_fusion.2
  147.3 0.2 select_subtract_fusion.47
  157.5 0.3 convolution_bitcast_fusion.2
  157.8 0.3 fusion.4
  158.1 0.3 fusion.135
  158.3 0.4 fusion.3
  158.7 1.5 gather_fusion.3
  160.3 0.6 reduce_sum.103
  161.5 0.6 select_reduce_fusion.1
  162.8 0.2 select_subtract_fusion.23
  173.0 0.3 convolution_bitcast_fusion.1
  173.3 0.8 maximum_bitcast_fusion
  (213 shorter events, 39.7 us)
Async XLA Ops:
  7.2 100.0 %copy-start.1 = (s32[1,1,128]{2,1,0:T(1,128)S(1)}, s32[1,1,128]{2,1,0:T(1,128)}, u32[]{:S(2)}) copy-start(s32[1,1,128]{2,1,0:T(1,128)} %param.12) | copy-start | bytes 1540
  7.2 77.3 %all-gather.2.cloned.1.call-start = ((), (), s32[]{:S(2)}) async-start(), calls=%async_computation.1 | async-start | bytes 8454144 | tf_op jit(solution)/shard_map/all_gather | solution.py:62
  91.3 15.4 %all-to-all-start = ((bf16[128,2,256]{2,1,0:T(2,128)(2,1)}), bf16[128,2,256]{2,1,0:T(2,128)(2,1)S(1)}, u32[]{:S(2)}, u32[]{:S(2)}) async-start(bf16[128,2,256]{2,1,0:T(2,128)(2,1)} %reshape.69), calls=%async_computation | async-start | bytes 262144 | tf_op jit(solution)/shard_map/all_to_all | solution.py:79
  107.7 17.5 %collective-permute-start = (f32[128,256]{1,0:T(8,128)S(1)}, f32[128,256]{1,0:T(8,128)S(1)}, u32[]{:S(2)}, u32[]{:S(2)}) collective-permute-start(f32[128,256]{1,0:T(8,128)S(1)} %fusion.1), channel_id=1, source_target_pairs={{0,1},{1,0},{2,3},{3,2},{4,5},{5,4},{6,7},{7,6},{8,9},{9,8},{10,11... | collective-permute-start | bytes 393224 | tf_op jit(solution)/shard_map/ppermute | solution.py:17
  126.1 15.7 %collective-permute-start.1 = (f32[128,256]{1,0:T(8,128)S(1)}, f32[128,256]{1,0:T(8,128)S(1)}, u32[]{:S(2)}, u32[]{:S(2)}) collective-permute-start(f32[128,256]{1,0:T(8,128)S(1)} %fusion.8), channel_id=1, source_target_pairs={{0,2},{2,0},{1,3},{3,1},{4,6},{6,4},{5,7},{7,5},{8,10},{10,8},{9,1... | collective-permute-start | bytes 393224 | tf_op jit(solution)/shard_map/ppermute | solution.py:17
  142.7 15.0 %collective-permute-start.2 = (f32[128,256]{1,0:T(8,128)S(1)}, f32[128,256]{1,0:T(8,128)S(1)}, u32[]{:S(2)}, u32[]{:S(2)}) collective-permute-start(f32[128,256]{1,0:T(8,128)S(1)} %fusion.6), channel_id=1, source_target_pairs={{0,4},{4,0},{1,5},{5,1},{2,6},{6,2},{3,7},{7,3},{8,12},{12,8},{9,1... | collective-permute-start | bytes 393224 | tf_op jit(solution)/shard_map/ppermute | solution.py:17
  158.1 16.0 %copy-start = (f32[128,256]{1,0:T(8,128)}, f32[128,256]{1,0:T(8,128)S(1)}, u32[]{:S(2)}) copy-start(f32[128,256]{1,0:T(8,128)S(1)} %fusion.4) | copy-start | bytes 393220
Sparse Core Ops, SparseCore 0:
  11.1 73.3 all-gather.1
where the time goes:
time: 181 us
  waiting for transfers between devices  81.5 us (45%)
  matrix products  52.4 us (29%)
  between operations  21.9 us (12%)
  local copies, waits for them, and re-layouts  8.81 us (5%)
  starting transfers between devices  8.28 us (5%)
  other arithmetic  8.05 us (4%)
    all_gather x1, waiting for transfers between devices, local(): lax.all_gather(sketch_matrix, ('front', 'grp'), axis=0, tiled=True)  71.7 us
    dot_general x96, matrix products, ridge_map(): jnp.dot(gram, approx, precision=lax.Precision.HIGHEST)  19.7 us
    dot_general x96, matrix products, ridge_map(): jnp.dot(approx, 2.0 * ident - jnp.dot(gram, approx, precision=lax.Precisi...  19.5 us
    all_to_all x1, waiting for transfers between devices, local(): lax.all_to_all(packed, ('front', 'grp'), split_axis=0, concat_axis=0, til...  9.02 us
    dot_general x1, matrix products, local(): jnp.dot(placing, sketch, preferred_element_type=jnp.float32)  6.12 us
    all_to_all x1, starting transfers between devices, local(): lax.all_to_all(packed, ('front', 'grp'), split_axis=0, concat_axis=0, til...  5.37 us
    gather x4, local copies, waits for them, and re-layouts, ridge_map(): shift = 0.1 * jnp.mean(jnp.diagonal(gram)) + 1e-05  5.28 us
  transfers between devices with their start and end apart: 5, of which 2 were waited for; matrix products, arithmetic and copies ran while one was open for 25% of the time, Pallas kernels for 0%

commit v1 on v0

--- a/solution.py
+++ b/solution.py
@@ -57,9 +57,18 @@
     rows_dev = contributions.shape[0]
     width = sketch_matrix.shape[1]
     capacity = 2 * rows_dev // devices
+    divide_results = lambda array_in, axis_name: jnp.concatenate(
+        lax.all_to_all(
+            jnp.stack([array_in] * lax.axis_size(axis_name), 0),
+            axis_name,
+            split_axis=0,
+            concat_axis=0,
+        ),
+        axis=0,
+    )
     sketch = jnp.dot(
         contributions,
-        lax.all_gather(sketch_matrix, ("front", "grp"), axis=0, tiled=True),
+        divide_results(sketch_matrix, ("front", "grp")),
         preferred_element_type=jnp.float32,
     )
     sketch = sketch.astype(jnp.bfloat16)

time: 181 us -> 217 us (1.20)
  waiting for transfers between devices: 81.5 us -> 113 us
  starting transfers between devices: 8.28 us -> 23.7 us
  between operations: 21.9 us -> 8.56 us
  local copies, waits for them, and re-layouts: 8.81 us -> 12.4 us
    all_to_all x0 -> x1, waiting for transfers between devices: none -> 104 us  [local(): lax.all_to_all(jnp.stack([array_in] * lax.axis_size(axis_name), 0), axis_...]
    all_gather x1 -> x0, waiting for transfers between devices: 71.7 us -> none  [local(): lax.all_gather(sketch_matrix, ('front', 'grp'), axis=0, tiled=True)]
    all_to_all x0 -> x1, starting transfers between devices: none -> 11.9 us  [local(): lax.all_to_all(jnp.stack([array_in] * lax.axis_size(axis_name), 0), axis_...]
    another operation x0 -> x1, local copies, waits for them, and re-layouts: none -> 5.09 us  [local(): jnp.stack([array_in] * lax.axis_size(axis_name), 0)]
    all_to_all x1, starting transfers between devices: 5.37 us -> 8.89 us  [local(): lax.all_to_all(packed, ('front', 'grp'), split_axis=0, concat_axis=0, til...]
  transfers between devices with their start and end apart: 5 -> 5, of which waited for: 2 -> 2; matrix products, arithmetic and copies ran while one was open for 25% -> 19% of each run, Pallas kernels for 0% -> 0%
where the time goes in v1:
time: 217 us; the launch traced here: 216 us
  waiting for transfers between devices  113 us (52%)
  matrix products  52.4 us (24%)
  starting transfers between devices  23.7 us (11%)
  local copies, waits for them, and re-layouts  12.4 us (6%)
  between operations  8.56 us (4%)
  other arithmetic  6.52 us (3%)
    all_to_all x1, waiting for transfers between devices, local(): lax.all_to_all(jnp.stack([array_in] * lax.axis_size(axis_name), 0), axis_...  104 us
    dot_general x96, matrix products, ridge_map(): jnp.dot(gram, approx, precision=lax.Precision.HIGHEST)  19.7 us
    dot_general x96, matrix products, ridge_map(): jnp.dot(approx, 2.0 * ident - jnp.dot(gram, approx, precision=lax.Precisi...  19.5 us
    all_to_all x1, starting transfers between devices, local(): lax.all_to_all(jnp.stack([array_in] * lax.axis_size(axis_name), 0), axis_...  11.9 us
    all_to_all x1, waiting for transfers between devices, local(): lax.all_to_all(packed, ('front', 'grp'), split_axis=0, concat_axis=0, til...  9.02 us
    all_to_all x1, starting transfers between devices, local(): lax.all_to_all(packed, ('front', 'grp'), split_axis=0, concat_axis=0, til...  8.89 us
    dot_general x1, matrix products, local(): jnp.dot(placing, sketch, preferred_element_type=jnp.float32)  6.12 us
    gather x4, local copies, waits for them, and re-layouts, ridge_map(): shift = 0.1 * jnp.mean(jnp.diagonal(gram)) + 1e-05  5.28 us
  transfers between devices with their start and end apart: 5, of which 2 were waited for; matrix products, arithmetic and copies ran while one was open for 19% of the time, Pallas kernels for 0%

profile of v1, /device:TPU:1, one launch (start us, length us, event | category | flops | bytes accessed | tf_op | source)
XLA Modules:
  0.0 216.2 jit_solution(8791549030148630801)
XLA Ops:
  0.6 5.1 %stack.10 = bf16[128,128,256]{2,1,0:T(8,128)(2,1)} broadcast(bf16[128,256]{1,0:T(8,128)(2,1)} %param.8), dimensions={1,2} | broadcast | bytes 8454144 | tf_op jit(solution)/shard_map/stack | solution.py:62
  5.7 11.9 %all-to-all-start = ((bf16[128,128,256]{2,1,0:T(8,128)(2,1)}), bf16[128,128,256]{2,1,0:T(8,128)(2,1)}, u32[]{:S(2)}, u32[]{:S(2)}) async-start(bf16[128,128,256]{2,1,0:T(8,128)(2,1)} %stack.10), calls=%async_computation | async-start | bytes 16777216 | tf_op jit(solution)/shard_map/all_to_all | solution.py:61
  19.5 103.6 %all-to-all-done = bf16[128,128,256]{2,1,0:T(8,128)(2,1)} async-done(((bf16[128,128,256]{2,1,0:T(8,128)(2,1)}), bf16[128,128,256]{2,1,0:T(8,128)(2,1)}, u32[]{:S(2)}, u32[]{:S(2)}) %all-to-all-start) | async-done | bytes 8388640 | tf_op jit(solution)/shard_map/all_to_all | solution.py:61
  123.1 6.1 %convolution_convert_fusion = bf16[256,256]{1,0:T(8,128)(2,1)S(1)} fusion(bf16[128,16384]{1,0:T(8,128)(2,1)} %param.7, bf16[16384,256]{1,0:T(8,128)(2,1)} %bitcast.6, s32[128]{0:T(128)S(1)} %fusion.46), kind=kOutput, calls=%fused_computation.102 | convolution fusion | flops 1090650112 | bytes 12714496 | tf_op jit(solution)/shard_map/dot_general | solution.py:86
  129.2 0.7 reshape.75
  129.9 8.9 %all-to-all-start.1 = ((bf16[128,2,256]{2,1,0:T(2,128)(2,1)}), bf16[128,2,256]{2,1,0:T(2,128)(2,1)S(1)}, u32[]{:S(2)}, u32[]{:S(2)}) async-start(bf16[128,2,256]{2,1,0:T(2,128)(2,1)} %reshape.75), calls=%async_computation.1 | async-start | bytes 262144 | tf_op jit(solution)/shard_map/all_to_all | solution.py:88
  139.1 0.7 fusion.43
  139.8 9.0 %all-to-all-done.1 = bf16[128,2,256]{2,1,0:T(2,128)(2,1)S(1)} async-done(((bf16[128,2,256]{2,1,0:T(2,128)(2,1)}), bf16[128,2,256]{2,1,0:T(2,128)(2,1)S(1)}, u32[]{:S(2)}, u32[]{:S(2)}) %all-to-all-start.1) | async-done | bytes 131104 | tf_op jit(solution)/shard_map/all_to_all | solution.py:88
  148.9 0.3 convolution_select_fusion
  149.2 0.6 fusion.1
  149.8 1.0 fusion.62
  150.8 0.3 fusion.63
  151.1 0.8 collective-permute-start
  151.9 1.2 gather_fusion
  153.1 0.6 reduce_sum.97
  154.4 0.6 select_reduce_fusion.4
  155.7 0.2 select_subtract_fusion.95
  157.0 0.2 select_subtract_fusion.92
  157.8 0.2 select_subtract_fusion.90
  159.9 0.2 select_subtract_fusion.85
  165.9 1.4 convolution_bitcast_fusion
  167.3 0.3 fusion.8
  167.6 1.4 collective-permute-start.1
  168.9 0.4 fusion.7
  169.3 0.3 fusion.87
  169.6 1.2 gather_fusion.1
  170.8 0.6 reduce_sum.99
  172.1 0.6 select_reduce_fusion.3
  173.4 0.2 select_subtract_fusion.71
  183.6 0.3 convolution_bitcast_fusion.3
  183.9 0.3 fusion.6
  184.2 0.7 collective-permute-start.2
  184.9 0.4 fusion.5
  185.3 0.3 fusion.111
  185.5 1.2 gather_fusion.2
  186.8 0.6 reduce_sum.101
  188.1 0.6 select_reduce_fusion.2
  189.4 0.2 select_subtract_fusion.47
  199.6 0.3 convolution_bitcast_fusion.2
  199.9 0.3 fusion.4
  200.2 0.4 fusion.3
  200.5 0.3 fusion.135
  200.8 1.5 gather_fusion.3
  202.4 0.6 reduce_sum.103
  203.6 0.6 select_reduce_fusion.1
  204.9 0.2 select_subtract_fusion.23
  215.1 0.3 convolution_bitcast_fusion.1
  215.4 0.8 maximum_bitcast_fusion
  (217 shorter events, 39.3 us)
Async XLA Ops:
  5.7 12.0 %copy-start.1 = (s32[16384,1]{0,1:T(1,128)S(1)}, s32[16384,1]{0,1:T(1,128)}, u32[]{:S(2)}) copy-start(s32[16384,1]{0,1:T(1,128)} %param.9) | copy-start | bytes 196612
  5.7 13.6 %copy-start.2 = (s32[16384]{0:T(1024)S(1)}, s32[16384]{0:T(1024)}, u32[]{:S(2)}) copy-start(s32[16384]{0:T(1024)} %param.10) | copy-start | bytes 196612
  5.7 117.4 %all-to-all-start = ((bf16[128,128,256]{2,1,0:T(8,128)(2,1)}), bf16[128,128,256]{2,1,0:T(8,128)(2,1)}, u32[]{:S(2)}, u32[]{:S(2)}) async-start(bf16[128,128,256]{2,1,0:T(8,128)(2,1)} %stack.10), calls=%async_computation | async-start | bytes 16777216 | tf_op jit(solution)/shard_map/all_to_all | solution.py:61
  17.7 131.5 %copy-start.3 = (s32[1,1,128]{2,1,0:T(1,128)S(1)}, s32[1,1,128]{2,1,0:T(1,128)}, u32[]{:S(2)}) copy-start(s32[1,1,128]{2,1,0:T(1,128)} %param.12) | copy-start | bytes 1540
  129.9 18.9 %all-to-all-start.1 = ((bf16[128,2,256]{2,1,0:T(2,128)(2,1)}), bf16[128,2,256]{2,1,0:T(2,128)(2,1)S(1)}, u32[]{:S(2)}, u32[]{:S(2)}) async-start(bf16[128,2,256]{2,1,0:T(2,128)(2,1)} %reshape.75), calls=%async_computation.1 | async-start | bytes 262144 | tf_op jit(solution)/shard_map/all_to_all | solution.py:88
  151.1 16.2 %collective-permute-start = (f32[128,256]{1,0:T(8,128)S(1)}, f32[128,256]{1,0:T(8,128)S(1)}, u32[]{:S(2)}, u32[]{:S(2)}) collective-permute-start(f32[128,256]{1,0:T(8,128)S(1)} %fusion.1), channel_id=1, source_target_pairs={{0,1},{1,0},{2,3},{3,2},{4,5},{5,4},{6,7},{7,6},{8,9},{9,8},{10,11... | collective-permute-start | bytes 393224 | tf_op jit(solution)/shard_map/ppermute | solution.py:17
  167.6 16.3 %collective-permute-start.1 = (f32[128,256]{1,0:T(8,128)S(1)}, f32[128,256]{1,0:T(8,128)S(1)}, u32[]{:S(2)}, u32[]{:S(2)}) collective-permute-start(f32[128,256]{1,0:T(8,128)S(1)} %fusion.8), channel_id=1, source_target_pairs={{0,2},{2,0},{1,3},{3,1},{4,6},{6,4},{5,7},{7,5},{8,10},{10,8},{9,1... | collective-permute-start | bytes 393224 | tf_op jit(solution)/shard_map/ppermute | solution.py:17
  184.2 15.7 %collective-permute-start.2 = (f32[128,256]{1,0:T(8,128)S(1)}, f32[128,256]{1,0:T(8,128)S(1)}, u32[]{:S(2)}, u32[]{:S(2)}) collective-permute-start(f32[128,256]{1,0:T(8,128)S(1)} %fusion.6), channel_id=1, source_target_pairs={{0,4},{4,0},{1,5},{5,1},{2,6},{6,2},{3,7},{7,3},{8,12},{12,8},{9,1... | collective-permute-start | bytes 393224 | tf_op jit(solution)/shard_map/ppermute | solution.py:17
  200.1 16.0 %copy-start = (f32[128,256]{1,0:T(8,128)}, f32[128,256]{1,0:T(8,128)S(1)}, u32[]{:S(2)}) copy-start(f32[128,256]{1,0:T(8,128)S(1)} %fusion.4) | copy-start | bytes 393220
